TPU v7x, 32 devices: a whole 2x2x4 slice. The times are simulated.
32 devices in a mesh: freq: 4 (over y, x), ma: 8 (over z, core).
Axes of the slice: x: 2, y: 2, z: 4, core: 2. Of those that a mesh axis runs over, the one named last changes fastest.
Arguments:
- sky_coeffs: bfloat16 [4, 2, 3, 256, 8, 16, 128], P('freq', None, None, None, 'ma'), may hold values from -6 to 6
- beam_transfer: bfloat16 [4, 8, 2, 3, 2048, 512], P('freq', 'ma'), may hold values from -0.078125 to 0.078125
- svd_basis: bfloat16 [4, 16, 2, 256, 512], P('freq', 'ma'), may hold values from -0.1875 to 0.1875
- kl_basis: bfloat16 [16, 2, 256, 4, 256], P('ma'), may hold values from -0.1875 to 0.1875
- m_values: int32 [16], P('ma'), may hold values from 1 to 2047, as said below
- svd_count: int32 [16], P('ma'), may hold values from 128 to 256, as said below
- kl_index: int32 [16, 128], P('ma'), may hold values from 0 to 255, as said below
- kl_count: int32 [16], P('ma'), may hold values from 64 to 128, as said below
Outputs:
- kl_modes: bfloat16 [16, 2, 128, 128], P('ma', None, None, 'freq')
Inputs may be any that keep to these rules, and one draw needn't show every extreme that they name: `m_values`: for each owner, the sum of 2048 - m over its 2 m-values is at most 2048, and equals 2048 for owner 0. `svd_count`: slot 0 retains all 256 modes. `kl_index`: entries of one m are distinct. `kl_count`: slot 0 retains all 128 modes.
All inputs are finite; a program needn't handle non-finite values.
Results may differ from a plain program's by a relative error of at most 0.012.
Values may be sent and summed in bfloat16 or wider, within the bound.
A program may use at most 128 MiB of HBM per device.

v0:
```python
import jax
import jax.numpy as jnp
from jax import lax
from jax.sharding import PartitionSpec as P


def pack_rows(sky_freq, m_owner):
    multipoles = sky_freq.shape[2]
    padded = jnp.pad(sky_freq, ((0, 0), (0, 0), (multipoles, multipoles), (0, 0), (0, 0)))
    row_index = jnp.arange(multipoles, dtype=jnp.int32)
    row_start = jnp.zeros((), jnp.int32)
    packed_list = []
    for slot_num in range(sky_freq.shape[3]):
        span_len = multipoles - m_owner[slot_num]
        row_shift = m_owner[slot_num] - row_start
        shifted = lax.dynamic_slice_in_dim(
            padded[:, :, :, slot_num, :], multipoles + row_shift, multipoles, 2
        )
        row_mask = (row_index >= row_start) & (row_index < row_start + span_len)
        packed_list.append(
            jnp.where(row_mask[None, None, :, None], shifted, jnp.zeros((), shifted.dtype))
        )
        row_start = row_start + span_len
    return jnp.stack(packed_list, 3)


def complex_stack(first_part, second_part):
    return jnp.stack([jnp.stack([first_part, -second_part]), jnp.stack([second_part, first_part])])


def shards(sky_coeffs, beam_transfer, svd_basis, kl_basis, m_values, svd_count, kl_index, kl_count):
    beam_owner = beam_transfer[0, 0]
    svd_owner = svd_basis[0]
    mode_total = svd_owner.shape[2]
    whole = lax.all_to_all(sky_coeffs, "ma", split_axis=5, concat_axis=4, tiled=True)[0]
    merged = whole.reshape(
        2, whole.shape[1], whole.shape[2] * whole.shape[3], whole.shape[4], whole.shape[5]
    )
    packed = pack_rows(merged, m_values)
    stacked = complex_stack(packed[0], packed[1])
    visibility = lax.dot_general(
        stacked, beam_owner, (((1, 2, 3), (0, 1, 2)), ((), ())), preferred_element_type=jnp.float32
    ).astype(jnp.bfloat16)
    rotated = jnp.stack(
        [jnp.stack([visibility[0], visibility[1]]), jnp.stack([visibility[1], -visibility[0]])]
    )
    coefficients = jnp.einsum(
        "oqsrb,sqjb->osjr", rotated, svd_owner, preferred_element_type=jnp.float32
    )
    mode_mask = jnp.arange(mode_total, dtype=jnp.int32)[None, :] < svd_count[:, None]
    coefficients = jnp.where(mode_mask[None, :, :, None], coefficients, 0.0).astype(jnp.bfloat16)
    selected = jax.vmap(lambda basis_one, chosen: jnp.take(basis_one, chosen, axis=1))(
        kl_basis, kl_index
    )
    keep_mask = jnp.arange(selected.shape[2], dtype=jnp.int32)[None, :] < kl_count[:, None]
    spread = lax.all_to_all(
        coefficients[:, :, None], "freq", split_axis=4, concat_axis=2, tiled=True
    )
    stacked = complex_stack(spread[0], spread[1])
    kl_out = jnp.einsum("oqsfjr,sqifj->soir", stacked, selected, preferred_element_type=jnp.float32)
    kl_out = jnp.where(keep_mask[:, None, :, None], kl_out, 0.0)
    return kl_out.astype(jnp.bfloat16)


def solution(mesh):
    return jax.shard_map(
        shards,
        mesh=mesh,
        in_specs=(
            P("freq", None, None, None, "ma", None, None),
            P("freq", "ma", None, None, None, None),
            P("freq", "ma", None, None, None),
            P("ma", None, None, None, None),
            P("ma"),
            P("ma"),
            P("ma", None),
            P("ma"),
        ),
        out_specs=P("ma", None, None, "freq"),
        check_vma=False,
    )
```

profile of v0, /device:TPU:0, one launch (start us, length us, event | category | flops | bytes accessed | tf_op | source)
XLA Modules:
  0.0 216.5 jit_solution(16721079827278895955)
XLA Ops:
  0.0 0.0 copy-start
  0.0 7.2 %copy.20 = bf16[1,2,3,256,1,16,128]{6,3,2,1,4,0,5:T(8,128)(2,1)} copy(bf16[1,2,3,256,1,16,128]{6,5,4,3,2,1,0:T(8,128)(2,1)} %param.8) | data formatting | bytes 12582912 | tf_op args[0]
  7.2 6.5 %all-to-all-start = ((bf16[1,2,3,256,1,16,128]{6,3,2,1,4,0,5:T(8,128)(2,1)}), bf16[1,2,3,256,1,16,128]{6,3,2,1,4,0,5:T(8,128)(2,1)}, u32[]{:S(2)}, u32[]{:S(2)}) async-start(bf16[1,2,3,256,1,16,128]{6,3,2,1,4,0,5:T(8,128)(2,1)} %copy.20), calls=%async_computation | async-start | bytes 12582912 | tf_op jit(solution)/shard_map/all_to_all | solution.py:35
  13.7 0.0 copy-done.4
  13.7 0.6 fusion.38
  17.3 0.0 copy-done.3
  17.3 0.0 copy-done
  17.3 2.9 %gather_fusion = bf16[256,2,4,256]{3,2,1,0:T(4,128)(2,1)} fusion(bf16[2,2,256,4,256]{4,3,2,1,0:T(4,128)(2,1)S(1)} %copy-done, s32[256]{0:T(256)S(1)} %fusion.31), kind=kCustom, calls=%fused_computation | custom fusion | bytes 2099200 | tf_op jit(solution)/shard_map/vmap(jit(_take))/gather | solution.py:52
  20.2 0.0 copy-done.7
  20.3 0.1 iota_compare_fusion.3
  20.3 132.4 %all-to-all-done = bf16[1,2,3,256,1,16,128]{6,3,2,1,4,0,5:T(8,128)(2,1)} async-done(((bf16[1,2,3,256,1,16,128]{6,3,2,1,4,0,5:T(8,128)(2,1)}), bf16[1,2,3,256,1,16,128]{6,3,2,1,4,0,5:T(8,128)(2,1)}, u32[]{:S(2)}, u32[]{:S(2)}) %all-to-all-start) | async-done | bytes 6291488 | tf_op jit(solution)/shard_map/all_to_all | solution.py:35
  152.7 9.5 %copy.21 = bf16[1,2,3,256,1,16,128]{6,5,3,2,1,4,0:T(8,128)(2,1)} copy(bf16[1,2,3,256,1,16,128]{6,3,2,1,4,0,5:T(8,128)(2,1)} %all-to-all-done) | data formatting | bytes 12582912 | tf_op jit(solution)/shard_map/all_to_all | solution.py:35
  162.2 16.3 %copy.22 = bf16[2,3,2048,2,128]{2,4,1,0,3:T(8,128)(2,1)} copy(bf16[2,3,2048,2,128]{4,3,2,1,0:T(2,128)(2,1)} %bitcast.89) | data formatting | bytes 12582912 | tf_op jit(solution)/shard_map/reshape;squeeze | solution.py:36
  178.5 4.6 %pad_slice_fusion = (bf16[2,3,6144,1,128]{2,4,1,0,3:T(8,128)(2,1)S(1)}, bf16[2,3,6144,1,128]{2,4,1,0,3:T(8,128)(2,1)S(1)}) fusion(bf16[2,3,2048,2,128]{2,4,1,0,3:T(8,128)(2,1)} %copy.22), kind=kLoop, calls=%fused_computation.1 | loop fusion | bytes 25165824 | tf_op jit(solution)/shard_map/slice | solution.py:17
  183.1 6.4 %dynamic-slice_select_fusion = (bf16[2,3,2048,1,128]{2,4,1,0,3:T(8,128)(2,1)S(1)}, bf16[2,3,2048,1,128]{2,4,1,0,3:T(8,128)(2,1)}) fusion(bf16[2,3,6144,1,128]{2,4,1,0,3:T(8,128)(2,1)S(1)} %get-tuple-element.8, s32[]{:T(128)S(6)} %select_n.38, pred[2048]{0:T(1024)(128)(4,1)S(1)} %fusion.30, bf16[2,3,6144,1,128]{2,4,1,0,3:T(8,128)(2,1)S(1)} %get-tuple-element.9, ...), kind=kLoop, calls=%fused_computation.14 | loop fusion | flops 3145728 | bytes 12587016 | tf_op jit(solution)/shard_map/jit(_where)/select_n | solution.py:21
  189.5 2.2 %fusion.36 = (bf16[1,3,2048,2,128]{2,4,1,0,3:T(8,128)(2,1)S(1)}, bf16[1,3,2048,2,128]{2,4,1,0,3:T(8,128)(2,1)S(1)}, bf16[1,3,2048,2,128]{2,4,1,0,3:T(8,128)(2,1)S(1)}) fusion(bf16[2,3,2048,1,128]{2,4,1,0,3:T(8,128)(2,1)S(1)} %get-tuple-element.20, bf16[2,3,2048,1,128]{2,4,1,0,3:T(8,128)(2,1)} %get-tuple-element.21), kind=kLoop, calls=%fused_computation.56 | loop fusion | flops 4718592 | bytes 15728640 | tf_op jit(solution)/shard_map/neg | solution.py:28
  191.7 1.3 maximum_bitcast_fusion
  193.0 0.0 copy-start.6
  193.0 0.0 copy-start.1
  193.0 11.4 %fusion.11 = bf16[2,2,128,512]{3,2,1,0:T(8,128)(2,1)S(1)} fusion(bf16[1,1,2,3,2048,512]{5,4,3,2,1,0:T(8,128)(2,1)} %param.9, bf16[1,2,3,2048,2,128]{3,5,2,1,4,0:T(8,128)(2,1)S(1)} %get-tuple-element.11, bf16[1,2,3,2048,2,128]{3,5,2,1,4,0:T(8,128)(2,1)S(1)} %get-tuple-element.10), kind=kOutput, calls=%fused_computation.17 | convolution fusion | flops 6449004544 | bytes 25690112 | tf_op jit(solution)/shard_map/dot_general | solution.py:41
  204.4 0.0 copy-start.5
  204.4 0.0 copy-start.2
  204.5 0.1 maximum_bitcast_fusion.2
  204.5 0.0 copy-done.6
  204.5 0.5 fusion.18
  205.0 1.0 copy.24
  206.0 3.7 %all-to-all-start.1 = ((bf16[2,2,1,256,128]{3,0,1,2,4:T(2,128)(2,1)}), bf16[2,2,1,256,128]{3,0,1,2,4:T(2,128)(2,1)S(1)}, u32[]{:S(2)}, u32[]{:S(2)}) async-start(bf16[2,2,1,256,128]{3,0,1,2,4:T(2,128)(2,1)} %copy.24), calls=%async_computation.1 | async-start | bytes 524288 | tf_op jit(solution)/shard_map/all_to_all | solution.py:56
  209.7 0.0 copy-done.5
  209.7 0.1 compare_and_fusion
  209.8 5.3 %all-to-all-done.1 = bf16[2,2,1,256,128]{3,0,1,2,4:T(2,128)(2,1)S(1)} async-done(((bf16[2,2,1,256,128]{3,0,1,2,4:T(2,128)(2,1)}), bf16[2,2,1,256,128]{3,0,1,2,4:T(2,128)(2,1)S(1)}, u32[]{:S(2)}, u32[]{:S(2)}) %all-to-all-start.1) | async-done | bytes 262176 | tf_op jit(solution)/shard_map/all_to_all | solution.py:56
  215.2 0.0 copy-done.2
  215.2 1.3 fusion.21
  (12 shorter events, 0.2 us)
Async XLA Ops:
  0.0 17.3 %copy-start = (bf16[2,2,256,4,256]{4,3,2,1,0:T(4,128)(2,1)S(1)}, bf16[2,2,256,4,256]{4,3,2,1,0:T(4,128)(2,1)}, u32[]{:S(2)}) copy-start(bf16[2,2,256,4,256]{4,3,2,1,0:T(4,128)(2,1)} %param.11) | copy-start | bytes 6291460
  7.2 6.5 %copy-start.4 = (s32[2]{0:T(128)S(1)}, s32[2]{0:T(128)}, u32[]{:S(2)}) copy-start(s32[2]{0:T(128)} %param.12) | copy-start | bytes 28
  7.2 10.1 %copy-start.3 = (s32[2,128]{1,0:T(2,128)S(1)}, s32[2,128]{1,0:T(2,128)}, u32[]{:S(2)}) copy-start(s32[2,128]{1,0:T(2,128)} %param.14) | copy-start | bytes 3076
  7.2 13.0 %copy-start.7 = (s32[2]{0:T(128)S(1)}, s32[2]{0:T(128)}, u32[]{:S(2)}) copy-start(s32[2]{0:T(128)} %param.13) | copy-start | bytes 28
  7.2 145.5 %all-to-all-start = ((bf16[1,2,3,256,1,16,128]{6,3,2,1,4,0,5:T(8,128)(2,1)}), bf16[1,2,3,256,1,16,128]{6,3,2,1,4,0,5:T(8,128)(2,1)}, u32[]{:S(2)}, u32[]{:S(2)}) async-start(bf16[1,2,3,256,1,16,128]{6,3,2,1,4,0,5:T(8,128)(2,1)} %copy.20), calls=%async_computation | async-start | bytes 12582912 | tf_op jit(solution)/shard_map/all_to_all | solution.py:35
  193.0 11.5 %copy-start.6 = (bf16[1,2,2,256,512]{4,3,2,1,0:T(8,128)(2,1)S(1)}, bf16[1,2,2,256,512]{4,3,2,1,0:T(8,128)(2,1)}, u32[]{:S(2)}) copy-start(bf16[1,2,2,256,512]{4,3,2,1,0:T(8,128)(2,1)} %param.10) | copy-start | bytes 3145732
  193.0 23.5 %copy-start.1 = (bf16[2,2,256,4,256]{4,3,2,1,0:T(4,128)(2,1)S(1)}, bf16[2,2,256,4,256]{4,3,2,1,0:T(4,128)(2,1)}, u32[]{:S(2)}) copy-start(bf16[2,2,256,4,256]{4,3,2,1,0:T(4,128)(2,1)} %param.11) | copy-start | bytes 6291460
  204.4 5.3 %copy-start.5 = (s32[2]{0:T(128)S(1)}, s32[2]{0:T(128)}, u32[]{:S(2)}) copy-start(s32[2]{0:T(128)} %param.15) | copy-start | bytes 28
  204.4 10.8 %copy-start.2 = (bf16[256,2,4,256]{3,2,1,0:T(4,128)(2,1)S(1)}, bf16[256,2,4,256]{3,2,1,0:T(4,128)(2,1)}, u32[]{:S(2)}) copy-start(bf16[256,2,4,256]{3,2,1,0:T(4,128)(2,1)} %gather_fusion) | copy-start | bytes 3145732
  206.0 9.1 %all-to-all-start.1 = ((bf16[2,2,1,256,128]{3,0,1,2,4:T(2,128)(2,1)}), bf16[2,2,1,256,128]{3,0,1,2,4:T(2,128)(2,1)S(1)}, u32[]{:S(2)}, u32[]{:S(2)}) async-start(bf16[2,2,1,256,128]{3,0,1,2,4:T(2,128)(2,1)} %copy.24), calls=%async_computation.1 | async-start | bytes 524288 | tf_op jit(solution)/shard_map/all_to_all | solution.py:56
where the time goes:
time: 217 us; the launch traced here: 216 us
  waiting for transfers between devices  138 us (64%)
  local copies, waits for them, and re-layouts  42.1 us (19%)
  matrix products  13.1 us (6%)
  starting transfers between devices  10.2 us (5%)
  other arithmetic  10.2 us (5%)
  between operations  3.21 us (1%)
    all_to_all x1, waiting for transfers between devices, shards(): lax.all_to_all(sky_coeffs, 'ma', split_axis=5, concat_axis=4, tiled=True)[0]  132 us
    another operation x1, local copies, waits for them, and re-layouts, shards(): whole.reshape(2, whole.shape[1], whole.shape[2] * whole.shape[3], whole.s...  16.3 us
    dot_general x1, matrix products, shards(): lax.dot_general(stacked, beam_owner, (((1, 2, 3), (0, 1, 2)), ((), ())),...  11.4 us
    all_to_all x1, local copies, waits for them, and re-layouts, shards(): lax.all_to_all(sky_coeffs, 'ma', split_axis=5, concat_axis=4, tiled=True)[0]  9.45 us
    unnamed x17, local copies, waits for them, and re-layouts  7.23 us
    all_to_all x1, starting transfers between devices, shards(): lax.all_to_all(sky_coeffs, 'ma', split_axis=5, concat_axis=4, tiled=True)[0]  6.49 us
    select_n x1, other arithmetic, pack_rows(): jnp.where(row_mask[None, None, :, None], shifted, jnp.zeros((), shifted.d...  6.39 us
    all_to_all x1, waiting for transfers between devices, shards(): lax.all_to_all(coefficients[:, :, None], 'freq', split_axis=4, concat_axi...  5.3 us
  transfers between devices with their start and end apart: 2, of which 2 were waited for; matrix products, arithmetic and copies ran while one was open for 2% of the time, Pallas kernels for 0%

commit v1 on v0

--- a/solution.py
+++ b/solution.py
@@ -2,6 +2,22 @@
 import jax.numpy as jnp
 from jax import lax
 from jax.sharding import PartitionSpec as P
+
+
+def pairwise_exchange(shard, axis, split, join):
+    ways, here = (lax.axis_size(axis), lax.axis_index(axis))
+    width = shard.shape[split] // ways
+    dims = list(shard.shape)
+    dims[split] = width
+    height = dims[join]
+    dims[join] = height * ways
+    full = jnp.zeros(dims, shard.dtype)
+    for mask in range(ways):
+        part = lax.dynamic_slice_in_dim(shard, (here ^ mask) * width, width, axis=split)
+        if mask:
+            part = lax.ppermute(part, axis, [(d, d ^ mask) for d in range(ways)])
+        full = lax.dynamic_update_slice_in_dim(full, part, (here ^ mask) * height, axis=join)
+    return full
 
 
 def pack_rows(sky_freq, m_owner):
@@ -32,7 +48,7 @@
     beam_owner = beam_transfer[0, 0]
     svd_owner = svd_basis[0]
     mode_total = svd_owner.shape[2]
-    whole = lax.all_to_all(sky_coeffs, "ma", split_axis=5, concat_axis=4, tiled=True)[0]
+    whole = pairwise_exchange(sky_coeffs, "ma", 5, 4)[0]
     merged = whole.reshape(
         2, whole.shape[1], whole.shape[2] * whole.shape[3], whole.shape[4], whole.shape[5]
     )

time: 217 us -> 485 us (2.24); the launches traced: 216 us -> 476 us
  local copies, waits for them, and re-layouts: 42.1 us -> 393 us
  waiting for transfers between devices: 138 us -> 43.8 us
    dynamic_update_slice x0 -> x8, local copies, waits for them, and re-layouts: none -> 329 us  [pairwise_exchange(): lax.dynamic_update_slice_in_dim(full, part, (here ^ mask) * height, axis=...]
    all_to_all x1 -> x0, waiting for transfers between devices: 132 us -> none  [shards(): lax.all_to_all(sky_coeffs, 'ma', split_axis=5, concat_axis=4, tiled=True)[0]]
    ppermute x0 -> x7, waiting for transfers between devices: none -> 37.4 us  [pairwise_exchange(): part = lax.ppermute(part, axis, [(d, d ^ mask) for d in range(ways)])]
    ppermute x0 -> x7, local copies, waits for them, and re-layouts: none -> 16.7 us  [pairwise_exchange(): part = lax.ppermute(part, axis, [(d, d ^ mask) for d in range(ways)])]
    dynamic_slice x0 -> x1, local copies, waits for them, and re-layouts: none -> 13.3 us  [pairwise_exchange(): lax.dynamic_slice_in_dim(shard, (here ^ mask) * width, width, axis=split)]
    ppermute x0 -> x7, starting transfers between devices: none -> 9.92 us  [pairwise_exchange(): part = lax.ppermute(part, axis, [(d, d ^ mask) for d in range(ways)])]
    all_to_all x1 -> x0, local copies, waits for them, and re-layouts: 9.45 us -> none  [shards(): lax.all_to_all(sky_coeffs, 'ma', split_axis=5, concat_axis=4, tiled=True)[0]]
    another operation x1, local copies, waits for them, and re-layouts: 16.3 us -> 8.7 us  [shards(): whole.reshape(2, whole.shape[1], whole.shape[2] * whole.shape[3], whole.s...]
  transfers between devices with their start and end apart: 2 -> 8, of which waited for: 2 -> 2; matrix products, arithmetic and copies ran while one was open for 2% -> 67% of each run, Pallas kernels for 0% -> 0%
where the time goes in v1:
time: 485 us; the launch traced here: 476 us
  local copies, waits for them, and re-layouts  393 us (81%)
  waiting for transfers between devices  43.8 us (9%)
  starting transfers between devices  13.6 us (3%)
  matrix products  13.1 us (3%)
  other arithmetic  10 us (2%)
    dynamic_update_slice x8, local copies, waits for them, and re-layouts, pairwise_exchange(): lax.dynamic_update_slice_in_dim(full, part, (here ^ mask) * height, axis=...  329 us
    ppermute x7, waiting for transfers between devices, pairwise_exchange(): part = lax.ppermute(part, axis, [(d, d ^ mask) for d in range(ways)])  37.4 us
    ppermute x7, local copies, waits for them, and re-layouts, pairwise_exchange(): part = lax.ppermute(part, axis, [(d, d ^ mask) for d in range(ways)])  16.7 us
    dynamic_slice x1, local copies, waits for them, and re-layouts, pairwise_exchange(): lax.dynamic_slice_in_dim(shard, (here ^ mask) * width, width, axis=split)  13.3 us
    unnamed x26, local copies, waits for them, and re-layouts  11.7 us
    dot_general x1, matrix products, shards(): lax.dot_general(stacked, beam_owner, (((1, 2, 3), (0, 1, 2)), ((), ())),...  11.4 us
    ppermute x7, starting transfers between devices, pairwise_exchange(): part = lax.ppermute(part, axis, [(d, d ^ mask) for d in range(ways)])  9.92 us
  transfers between devices with their start and end apart: 8, of which 2 were waited for; matrix products, arithmetic and copies ran while one was open for 67% of the time, Pallas kernels for 0%

profile of v1, /device:TPU:0, one launch (start us, length us, event | category | flops | bytes accessed | tf_op | source)
XLA Modules:
  0.0 476.4 jit_solution(9223107548034870515)
XLA Ops:
  0.0 13.3 %constant_dynamic-slice_fusion = (bf16[1,2,3,256,1,2,128]{6,5,4,3,2,1,0:T(2,128)(2,1)S(1)}, bf16[1,2,3,256,1,2,128]{6,5,4,3,2,1,0:T(2,128)(2,1)S(1)}, bf16[1,2,3...) fusion(bf16[1,2,3,256,1,16,128]{6,5,4,3,2,1,0:T(8,128)(2,1)} %p, ...), kind=kLoop, calls=%fused_computation.47 | loop fusion | bytes 12582944 | tf_op jit(solution)/shard_map/dynamic_slice | solution.py:16
  15.8 2.6 collective-permute-start.1
  20.5 2.7 collective-permute-start.3
  24.2 2.2 copy.67
  27.5 3.5 collective-permute-start.5
  31.0 37.3 %collective-permute-done.1 = bf16[1,2,3,256,1,2,128]{6,3,5,4,2,1,0:T(8,128)(2,1)} collective-permute-done((bf16[1,2,3,256,1,2,128]{6,3,5,4,2,1,0:T(8,128)(2,1)}, bf16[1,2,3,256,1,2,128]{6,3,5,4,2,1,0:T(8,128)(2,1)}, u32[]{:S(2)}, u32[]{:S(2)}) %collective-permute-start.1) | collective-permute-done | bytes 786464 | tf_op jit(solution)/shard_map/ppermute | solution.py:18
  70.6 3.3 copy.61
  75.9 2.9 gather_fusion
  78.8 3.7 broadcast_in_dim.74
  82.5 41.1 %dynamic_update_slice.24 = bf16[1,2,3,256,8,2,128]{6,4,3,5,2,1,0:T(8,128)(2,1)} dynamic-update-slice(bf16[1,2,3,256,8,2,128]{6,4,3,5,2,1,0:T(8,128)(2,1)} %broadcast_in_dim.74, bf16[1,2,3,256,1,2,128]{6,4,3,5,2,1,0:T(2,128)(2,1)S(1)} %copy-done.2, s32[]{:T(128)} %constant.20.clone.1, s32[]{:T(128)} %constant.20.clone.1, s32[]{:T(128)} %constant.20.clone.1, s32[]{:T(128)} %constant.20.clone.1, ...) | dynamic-update-slice | bytes 1572868 | tf_op jit(solution)/shard_map/dynamic_update_slice | solution.py:19
  123.7 2.5 copy.37
  126.2 41.1 %dynamic_update_slice.25 = bf16[1,2,3,256,8,2,128]{6,4,3,5,2,1,0:T(8,128)(2,1)} dynamic-update-slice(bf16[1,2,3,256,8,2,128]{6,4,3,5,2,1,0:T(8,128)(2,1)} %dynamic_update_slice.24, bf16[1,2,3,256,1,2,128]{6,4,3,5,2,1,0:T(2,128)(2,1)S(1)} %copy.37, s32[]{:T(128)} %constant.20.clone.1, s32[]{:T(128)} %constant.20.clone.1, s32[]{:T(128)} %constant.20.clone.1, s32[]{:T(128)} %constant.20.clone.1, ...) | dynamic-update-slice | bytes 1572868 | tf_op jit(solution)/shard_map/dynamic_update_slice | solution.py:19
  167.4 2.5 copy.39
  169.9 41.3 %dynamic_update_slice.26 = bf16[1,2,3,256,8,2,128]{6,4,3,5,2,1,0:T(8,128)(2,1)} dynamic-update-slice(bf16[1,2,3,256,8,2,128]{6,4,3,5,2,1,0:T(8,128)(2,1)} %dynamic_update_slice.25, bf16[1,2,3,256,1,2,128]{6,4,3,5,2,1,0:T(2,128)(2,1)S(1)} %copy.39, s32[]{:T(128)} %constant.20.clone.1, s32[]{:T(128)} %constant.20.clone.1, s32[]{:T(128)} %constant.20.clone.1, s32[]{:T(128)} %constant.20.clone.1, ...) | dynamic-update-slice | bytes 1572868 | tf_op jit(solution)/shard_map/dynamic_update_slice | solution.py:19
  211.2 2.5 copy.41
  213.8 41.1 %dynamic_update_slice.27 = bf16[1,2,3,256,8,2,128]{6,4,3,5,2,1,0:T(8,128)(2,1)} dynamic-update-slice(bf16[1,2,3,256,8,2,128]{6,4,3,5,2,1,0:T(8,128)(2,1)} %dynamic_update_slice.26, bf16[1,2,3,256,1,2,128]{6,4,3,5,2,1,0:T(2,128)(2,1)S(1)} %copy.41, s32[]{:T(128)} %constant.20.clone.1, s32[]{:T(128)} %constant.20.clone.1, s32[]{:T(128)} %constant.20.clone.1, s32[]{:T(128)} %constant.20.clone.1, ...) | dynamic-update-slice | bytes 1572868 | tf_op jit(solution)/shard_map/dynamic_update_slice | solution.py:19
  254.9 2.5 copy.43
  257.5 41.1 %dynamic_update_slice.28 = bf16[1,2,3,256,8,2,128]{6,4,3,5,2,1,0:T(8,128)(2,1)} dynamic-update-slice(bf16[1,2,3,256,8,2,128]{6,4,3,5,2,1,0:T(8,128)(2,1)} %dynamic_update_slice.27, bf16[1,2,3,256,1,2,128]{6,4,3,5,2,1,0:T(2,128)(2,1)S(1)} %copy.43, s32[]{:T(128)} %constant.20.clone.1, s32[]{:T(128)} %constant.20.clone.1, s32[]{:T(128)} %constant.20.clone.1, s32[]{:T(128)} %constant.20.clone.1, ...) | dynamic-update-slice | bytes 1572868 | tf_op jit(solution)/shard_map/dynamic_update_slice | solution.py:19
  298.6 2.5 copy.45
  301.1 41.1 %dynamic_update_slice.29 = bf16[1,2,3,256,8,2,128]{6,4,3,5,2,1,0:T(8,128)(2,1)} dynamic-update-slice(bf16[1,2,3,256,8,2,128]{6,4,3,5,2,1,0:T(8,128)(2,1)} %dynamic_update_slice.28, bf16[1,2,3,256,1,2,128]{6,4,3,5,2,1,0:T(2,128)(2,1)S(1)} %copy.45, s32[]{:T(128)} %constant.20.clone.1, s32[]{:T(128)} %constant.20.clone.1, s32[]{:T(128)} %constant.20.clone.1, s32[]{:T(128)} %constant.20.clone.1, ...) | dynamic-update-slice | bytes 1572868 | tf_op jit(solution)/shard_map/dynamic_update_slice | solution.py:19
  342.3 2.5 copy.47
  344.8 41.1 %dynamic_update_slice.30 = bf16[1,2,3,256,8,2,128]{6,4,3,5,2,1,0:T(8,128)(2,1)} dynamic-update-slice(bf16[1,2,3,256,8,2,128]{6,4,3,5,2,1,0:T(8,128)(2,1)} %dynamic_update_slice.29, bf16[1,2,3,256,1,2,128]{6,4,3,5,2,1,0:T(2,128)(2,1)S(1)} %copy.47, s32[]{:T(128)} %constant.20.clone.1, s32[]{:T(128)} %constant.20.clone.1, s32[]{:T(128)} %constant.20.clone.1, s32[]{:T(128)} %constant.20.clone.1, ...) | dynamic-update-slice | bytes 1572868 | tf_op jit(solution)/shard_map/dynamic_update_slice | solution.py:19
  385.9 1.4 copy.49
  387.4 41.1 %dynamic_update_slice.31 = bf16[1,2,3,256,8,2,128]{6,4,3,5,2,1,0:T(8,128)(2,1)} dynamic-update-slice(bf16[1,2,3,256,8,2,128]{6,4,3,5,2,1,0:T(8,128)(2,1)} %dynamic_update_slice.30, bf16[1,2,3,256,1,2,128]{6,4,3,5,2,1,0:T(2,128)(2,1)S(1)} %copy.49, s32[]{:T(128)} %constant.20.clone.1, s32[]{:T(128)} %constant.20.clone.1, s32[]{:T(128)} %constant.20.clone.1, s32[]{:T(128)} %constant.20.clone.1, ...) | dynamic-update-slice | bytes 1572868 | tf_op jit(solution)/shard_map/dynamic_update_slice | solution.py:19
  428.5 8.7 %copy.50 = bf16[2,3,2048,2,128]{2,4,1,0,3:T(8,128)(2,1)} copy(bf16[2,3,2048,2,128]{4,2,3,1,0:T(8,128)(2,1)} %bitcast.89) | data formatting | bytes 12582912 | tf_op jit(solution)/shard_map/reshape;squeeze | solution.py:52
  437.2 4.8 %pad_slice_fusion = (bf16[2,3,6144,1,128]{2,4,1,0,3:T(8,128)(2,1)S(1)}, bf16[2,3,6144,1,128]{2,4,1,0,3:T(8,128)(2,1)S(1)}) fusion(bf16[2,3,2048,2,128]{2,4,1,0,3:T(8,128)(2,1)} %copy.50), kind=kLoop, calls=%fused_computation.1 | loop fusion | bytes 25165824 | tf_op jit(solution)/shard_map/slice | solution.py:33
  442.0 6.4 %dynamic-slice_select_fusion = (bf16[2,3,2048,1,128]{2,4,1,0,3:T(8,128)(2,1)S(1)}, bf16[2,3,2048,1,128]{2,4,1,0,3:T(8,128)(2,1)}) fusion(bf16[2,3,6144,1,128]{2,4,1,0,3:T(8,128)(2,1)S(1)} %get-tuple-element.8, s32[]{:T(128)S(6)} %select_n.102, pred[2048]{0:T(1024)(128)(4,1)S(1)} %fusion.30, bf16[2,3,6144,1,128]{2,4,1,0,3:T(8,128)(2,1)S(1)} %get-tuple-element.9, ...), kind=kLoop, calls=%fused_computation.14 | loop fusion | flops 3145728 | bytes 12587016 | tf_op jit(solution)/shard_map/jit(_where)/select_n | solution.py:37
  448.4 2.2 fusion.36
  451.8 11.4 %fusion.11 = bf16[2,2,128,512]{3,2,1,0:T(8,128)(2,1)S(1)} fusion(bf16[1,1,2,3,2048,512]{5,4,3,2,1,0:T(8,128)(2,1)} %param.9, bf16[1,2,3,2048,2,128]{3,5,2,1,4,0:T(8,128)(2,1)S(1)} %get-tuple-element.19, bf16[1,2,3,2048,2,128]{3,5,2,1,4,0:T(8,128)(2,1)S(1)} %get-tuple-element.18), kind=kOutput, calls=%fused_computation.17 | convolution fusion | flops 6449004544 | bytes 25690112 | tf_op jit(solution)/shard_map/dot_general | solution.py:57
  464.7 3.7 all-to-all-start
  468.5 6.5 %all-to-all-done = bf16[2,2,1,256,128]{3,0,1,2,4:T(2,128)(2,1)S(1)} async-done(((bf16[2,2,1,256,128]{3,0,1,2,4:T(2,128)(2,1)}), bf16[2,2,1,256,128]{3,0,1,2,4:T(2,128)(2,1)S(1)}, u32[]{:S(2)}, u32[]{:S(2)}) %all-to-all-start) | async-done | bytes 262176 | tf_op jit(solution)/shard_map/all_to_all | solution.py:72
  475.1 1.3 fusion.21
  (49 shorter events, 10.9 us)
Async XLA Ops:
  0.0 75.9 %copy-start = (bf16[2,2,256,4,256]{4,3,2,1,0:T(4,128)(2,1)S(1)}, bf16[2,2,256,4,256]{4,3,2,1,0:T(4,128)(2,1)}, u32[]{:S(2)}) copy-start(bf16[2,2,256,4,256]{4,3,2,1,0:T(4,128)(2,1)} %param.11) | copy-start | bytes 6291460
  13.3 55.6 %copy-start.5 = (s32[2]{0:T(128)S(1)}, s32[2]{0:T(128)}, u32[]{:S(2)}) copy-start(s32[2]{0:T(128)} %param.12) | copy-start | bytes 28
  14.3 61.6 %copy-start.4 = (s32[2,128]{1,0:T(2,128)S(1)}, s32[2,128]{1,0:T(2,128)}, u32[]{:S(2)}) copy-start(s32[2,128]{1,0:T(2,128)} %param.14) | copy-start | bytes 3076
  14.3 13.2 %collective-permute-start = (bf16[1,2,3,256,1,2,128]{6,3,5,4,2,1,0:T(8,128)(2,1)}, bf16[1,2,3,256,1,2,128]{6,3,5,4,2,1,0:T(8,128)(2,1)}, u32[]{:S(2)}, u32[]{:S(2)}) collective-permute-start(bf16[1,2,3,256,1,2,128]{6,3,5,4,2,1,0:T(8,128)(2,1)} %copy.62), channel_id=1, source_target_pairs={{0,1},{1,0},{2,3},{3,2},{4,5},{5,4},{6,7},{7,6},{8,9},{9,8},{10,11... | collective-permute-start | bytes 2359304 | tf_op jit(solution)/shard_map/ppermute | solution.py:18
  15.8 52.5 %collective-permute-start.1 = (bf16[1,2,3,256,1,2,128]{6,3,5,4,2,1,0:T(8,128)(2,1)}, bf16[1,2,3,256,1,2,128]{6,3,5,4,2,1,0:T(8,128)(2,1)}, u32[]{:S(2)}, u32[]{:S(2)}) collective-permute-start(bf16[1,2,3,256,1,2,128]{6,3,5,4,2,1,0:T(8,128)(2,1)} %copy.63), channel_id=1, source_target_pairs={{0,2},{1,3},{2,0},{3,1},{4,6},{5,7},{6,4},{7,5},{8,10},{9,11},{10,... | collective-permute-start | bytes 2359304 | tf_op jit(solution)/shard_map/ppermute | solution.py:18
  19.4 191.8 %collective-permute-start.2 = (bf16[1,2,3,256,1,2,128]{6,3,5,4,2,1,0:T(8,128)(2,1)}, bf16[1,2,3,256,1,2,128]{6,3,5,4,2,1,0:T(8,128)(2,1)}, u32[]{:S(2)}, u32[]{:S(2)}) collective-permute-start(bf16[1,2,3,256,1,2,128]{6,3,5,4,2,1,0:T(8,128)(2,1)} %copy.64), channel_id=1, source_target_pairs={{0,3},{1,2},{2,1},{3,0},{4,7},{5,6},{6,5},{7,4},{8,11},{9,10},{10,... | collective-permute-start | bytes 2359304 | tf_op jit(solution)/shard_map/ppermute | solution.py:18
  20.5 234.4 %collective-permute-start.3 = (bf16[1,2,3,256,1,2,128]{6,3,5,4,2,1,0:T(8,128)(2,1)}, bf16[1,2,3,256,1,2,128]{6,3,5,4,2,1,0:T(8,128)(2,1)}, u32[]{:S(2)}, u32[]{:S(2)}) collective-permute-start(bf16[1,2,3,256,1,2,128]{6,3,5,4,2,1,0:T(8,128)(2,1)} %copy.65), channel_id=1, source_target_pairs={{0,4},{1,5},{2,6},{3,7},{4,0},{5,1},{6,2},{7,3},{8,12},{9,13},{10,... | collective-permute-start | bytes 2359304 | tf_op jit(solution)/shard_map/ppermute | solution.py:18
  24.2 274.4 %collective-permute-start.4 = (bf16[1,2,3,256,1,2,128]{6,3,5,4,2,1,0:T(8,128)(2,1)}, bf16[1,2,3,256,1,2,128]{6,3,5,4,2,1,0:T(8,128)(2,1)}, u32[]{:S(2)}, u32[]{:S(2)}) collective-permute-start(bf16[1,2,3,256,1,2,128]{6,3,5,4,2,1,0:T(8,128)(2,1)} %copy.66), channel_id=1, source_target_pairs={{0,5},{1,4},{2,7},{3,6},{4,1},{5,0},{6,3},{7,2},{8,13},{9,12},{10,... | collective-permute-start | bytes 2359304 | tf_op jit(solution)/shard_map/ppermute | solution.py:18
  27.5 314.8 %collective-permute-start.5 = (bf16[1,2,3,256,1,2,128]{6,3,5,4,2,1,0:T(8,128)(2,1)}, bf16[1,2,3,256,1,2,128]{6,3,5,4,2,1,0:T(8,128)(2,1)}, u32[]{:S(2)}, u32[]{:S(2)}) collective-permute-start(bf16[1,2,3,256,1,2,128]{6,3,5,4,2,1,0:T(8,128)(2,1)} %copy.67), channel_id=1, source_target_pairs={{0,6},{1,7},{2,4},{3,5},{4,2},{5,3},{6,0},{7,1},{8,14},{9,15},{10,... | collective-permute-start | bytes 2359304 | tf_op jit(solution)/shard_map/ppermute | solution.py:18
  68.4 317.6 %collective-permute-start.6 = (bf16[1,2,3,256,1,2,128]{6,3,5,4,2,1,0:T(8,128)(2,1)}, bf16[1,2,3,256,1,2,128]{6,3,5,4,2,1,0:T(8,128)(2,1)S(1)}, u32[]{:S(2)}, u32[]{:S(2)}) collective-permute-start(bf16[1,2,3,256,1,2,128]{6,3,5,4,2,1,0:T(8,128)(2,1)} %copy.68), channel_id=1, source_target_pairs={{0,7},{1,6},{2,5},{3,4},{4,3},{5,2},{6,1},{7,0},{8,15},{9,14},{10,... | collective-permute-start | bytes 2359304 | tf_op jit(solution)/shard_map/ppermute | solution.py:18
  73.9 49.7 %copy-start.8 = (s32[2]{0:T(128)S(1)}, s32[2]{0:T(128)}, u32[]{:S(2)}) copy-start(s32[2]{0:T(128)} %param.13) | copy-start | bytes 28
  78.8 3.7 copy-start.2
  451.8 11.5 %copy-start.7 = (bf16[1,2,2,256,512]{4,3,2,1,0:T(8,128)(2,1)S(1)}, bf16[1,2,2,256,512]{4,3,2,1,0:T(8,128)(2,1)}, u32[]{:S(2)}) copy-start(bf16[1,2,2,256,512]{4,3,2,1,0:T(8,128)(2,1)} %param.10) | copy-start | bytes 3145732
  451.8 24.6 %copy-start.1 = (bf16[2,2,256,4,256]{4,3,2,1,0:T(4,128)(2,1)S(1)}, bf16[2,2,256,4,256]{4,3,2,1,0:T(4,128)(2,1)}, u32[]{:S(2)}) copy-start(bf16[2,2,256,4,256]{4,3,2,1,0:T(4,128)(2,1)} %param.11) | copy-start | bytes 6291460
  463.1 5.3 %copy-start.6 = (s32[2]{0:T(128)S(1)}, s32[2]{0:T(128)}, u32[]{:S(2)}) copy-start(s32[2]{0:T(128)} %param.15) | copy-start | bytes 28
  463.2 11.9 %copy-start.3 = (bf16[256,2,4,256]{3,2,1,0:T(4,128)(2,1)S(1)}, bf16[256,2,4,256]{3,2,1,0:T(4,128)(2,1)}, u32[]{:S(2)}) copy-start(bf16[256,2,4,256]{3,2,1,0:T(4,128)(2,1)} %gather_fusion) | copy-start | bytes 3145732
  464.7 10.2 %all-to-all-start = ((bf16[2,2,1,256,128]{3,0,1,2,4:T(2,128)(2,1)}), bf16[2,2,1,256,128]{3,0,1,2,4:T(2,128)(2,1)S(1)}, u32[]{:S(2)}, u32[]{:S(2)}) async-start(bf16[2,2,1,256,128]{3,0,1,2,4:T(2,128)(2,1)} %copy.52), calls=%async_computation | async-start | bytes 524288 | tf_op jit(solution)/shard_map/all_to_all | solution.py:72
